TPU v7x, 32 devices: a whole 2x2x4 slice. The times are simulated.
32 devices in a mesh: img: 16 (over z, y, x), blk: 2 (over core).
Axes of the slice: x: 2, y: 2, z: 4, core: 2. Of those that a mesh axis runs over, the one named last changes fastest.
Arguments:
- descriptors: bfloat16 [64, 128, 256], P(('img', 'blk')), may hold values from -8 to 8
- covisible: int32 [64, 6], P(('img', 'blk')), may hold values from 0 to 63, as said below
- tile_counts: int32 [64], P(('img', 'blk')), may hold values from 1 to 6, as said below
- keypoints: int32 [64], replicated, may hold values from 32 to 128, as said below
- query_weight: bfloat16 [256, 256], replicated, may hold values from -0.375 to 0.375
- key_weight: bfloat16 [256, 256], replicated, may hold values from -0.375 to 0.375
- value_weight: bfloat16 [256, 256], replicated, may hold values from -0.375 to 0.375
- merge_weight: bfloat16 [512, 512], replicated, may hold values from -0.25 to 0.25
- output_weight: bfloat16 [512, 256], replicated, may hold values from -0.25 to 0.25
- dustbin: float32 [1], replicated, may hold values from 0.5 to 2
Outputs:
- plan: float32 [64, 6, 128, 128], P(('img', 'blk'))
- row_bin: float32 [64, 128], P(('img', 'blk'))
- col_bin: float32 [64, 128], P(('img', 'blk'))
Inputs may be any that keep to these rules, and one draw needn't show every extreme that they name: `covisible`: the 6 entries of a block's row name different blocks, never the block itself, all within its own image group of 4 consecutive blocks or the groups just before and after it. `tile_counts`: some block uses all 6 of its listed blocks. The valid keypoints of a block are its first ones; some block is full.
All inputs are finite; a program needn't handle non-finite values.
Results may differ from a plain program's by a relative error of at most 0.0032.
Values may be sent and summed in bfloat16 or wider, within the bound.
A program may use at most 64 MiB of HBM per device.

v0:
```python
import functools
import math

import jax
import jax.numpy as jnp
from jax import lax
from jax.experimental import pallas as pl
from jax.experimental.pallas import tpu as pltpu
from jax.sharding import PartitionSpec as P

HEADS = 4
ITERS = 3
DEAD = -1e30
MESH = pl.DeviceIdType.MESH


def kernel(
    img_count,
    blk_count,
    desc_in,
    cov_in,
    count_in,
    kpt_in,
    wq_in,
    wk_in,
    wv_in,
    wm_in,
    wo_in,
    dust_in,
    base_out,
    tail_ref,
    desc_ref,
    cov_ref,
    count_ref,
    kpt_ref,
    wq_ref,
    wk_ref,
    wv_ref,
    wm_ref,
    wo_ref,
    dust_ref,
    load_sem,
    base_sem,
    near_desc,
    near_ref,
    near_k,
    near_v,
    query,
    merged,
    scores,
    acc,
    mass_in,
    pot,
    desc_ssem,
    desc_rsem,
    ref_ssem,
    ref_rsem,
    mass_ssem,
    mass_rsem,
):
    local, block, width = desc_ref.shape
    tiles = cov_ref.shape[1]
    group = local * blk_count
    head_dim = width // HEADS
    img = lax.axis_index("img")
    blk = lax.axis_index("blk")
    others = [lax.rem(blk + step, blk_count) for step in range(1, blk_count)]
    first_block = (img - 1) * group

    def exists(shift):
        if shift == 0:
            return True
        return img + shift < img_count if shift > 0 else img + shift >= 0

    def guarded(shift, body):
        if shift == 0:
            body()
        else:
            pl.when(exists(shift))(body)

    pairs = (
        (desc_in, desc_ref),
        (wq_in, wq_ref),
        (wk_in, wk_ref),
        (wv_in, wv_ref),
        (wm_in, wm_ref),
        (cov_in, cov_ref),
        (count_in, count_ref),
        (kpt_in, kpt_ref),
        (dust_in, dust_ref),
        (wo_in, wo_ref),
    )
    loads = [
        pltpu.make_async_copy(source, target, load_sem.at[place])
        for place, (source, target) in enumerate(pairs)
    ]

    barrier = pltpu.get_barrier_semaphore()
    for shift in range(-2, 3):
        def greet(shift=shift):
            for member in others if shift == 0 else range(blk_count):
                pl.semaphore_signal(
                    barrier, inc=1, device_id=(img + shift, member), device_id_type=MESH
                )
        guarded(shift, greet)

    for load in loads:
        load.start()

    def slot(near, section, member):
        return near.at[pl.ds((section * blk_count + member) * local, local)]

    def sender(source, near, ssem, rsem, section, shift, member):
        return pltpu.make_async_remote_copy(
            src_ref=source,
            dst_ref=slot(near, section, blk),
            send_sem=ssem.at[section, member],
            recv_sem=rsem.at[section, blk],
            device_id=(img + shift, member),
            device_id_type=MESH,
        )

    def arrival(near, ssem, rsem, section, member):
        here = slot(near, section, member)
        return pltpu.make_async_remote_copy(
            src_ref=here,
            dst_ref=here,
            send_sem=ssem.at[section, member],
            recv_sem=rsem.at[section, member],
            device_id=(img, others[0]),
            device_id_type=MESH,
        )

    def send_own(source, near, ssem, rsem):
        for shift in (1, -1):
            guarded(
                shift,
                lambda shift=shift: sender(
                    source, near, ssem, rsem, 1 - shift, shift, blk
                ).start(),
            )
        for member in others:
            sender(source, near, ssem, rsem, 1, 0, member).start()

    def relay(near, ssem, rsem, section):
        def body():
            arrival(near, ssem, rsem, section, blk).wait_recv()
            for member in others:
                sender(slot(near, section, blk), near, ssem, rsem, section, 0, member).start()
        guarded(section - 1, body)

    def wait_relayed(near, ssem, rsem, section, after=None):
        def body():
            for member in others:
                arrival(near, ssem, rsem, section, member).wait_recv()
                if after is not None:
                    after(section, member)
        guarded(section - 1, body)

    def drain(source, near, ssem, rsem):
        for shift in (1, -1):
            guarded(
                shift,
                lambda shift=shift: sender(
                    source, near, ssem, rsem, 1 - shift, shift, blk
                ).wait_send(),
            )
        for section in range(3):
            def body(section=section):
                for member in others:
                    sender(source, near, ssem, rsem, section, 0, member).wait_send()
            guarded(section - 1, body)

    def project(rows, section, member):
        where_to = pl.ds((section * blk_count + member) * local, local)
        for weight, target in ((wk_ref, near_k), (wv_ref, near_v)):
            out = jnp.dot(rows, weight[...], preferred_element_type=jnp.float32)
            target[where_to] = out.astype(jnp.bfloat16).reshape(local, block, width)

    def project_near(section, member):
        rows = near_desc[pl.ds((section * blk_count + member) * local, local)]
        project(rows.reshape(local * block, width), section, member)

    for source in range(-2, 3):
        if source != 0:
            @pl.when(jnp.logical_not(exists(source)))
            def _(source=source):
                for sweep in range(ITERS):
                    mass_in[sweep, source + 2] = jnp.zeros(mass_in.shape[2:], jnp.float32)

    low = jnp.maximum(img - 2, 0)
    high = jnp.minimum(img + 2, img_count - 1)
    pl.semaphore_wait(barrier, (high - low + 1) * blk_count - 1)
    send_own(desc_in, near_desc, desc_ssem, desc_rsem)
    for load in loads:
        load.wait()
    own = desc_ref[...].reshape(local * block, width)

    scaled = jnp.dot(own, wq_ref[...], preferred_element_type=jnp.float32) * (
        1.0 / math.sqrt(head_dim)
    )
    query[...] = scaled.astype(jnp.bfloat16).reshape(local, block, width)
    project(own, 1, blk)
    merged[...] = jnp.dot(
        own, wm_ref[pl.ds(0, width), :], preferred_element_type=jnp.float32
    ).reshape(merged.shape)
    wait_relayed(near_desc, desc_ssem, desc_rsem, 1, project_near)
    for section in (0, 2):
        relay(near_desc, desc_ssem, desc_rsem, section)
    for section in (0, 2):
        guarded(section - 1, lambda section=section: project_near(section, blk))
    for section in (0, 2):
        wait_relayed(near_desc, desc_ssem, desc_rsem, section, project_near)

    lanes = lax.broadcasted_iota(jnp.int32, (1, block), 1)
    rows_at = lax.broadcasted_iota(jnp.int32, (block, 1), 0)
    head_of = lax.broadcasted_iota(jnp.int32, (1, width), 1) // head_dim
    heads = [head_of == head for head in range(HEADS)]
    own_kpt = [kpt_ref[(img * blk_count + blk) * local + r] for r in range(local)]
    near_ids = [
        [jnp.clip(cov_ref[r, t] - first_block, 0, 3 * group - 1) for t in range(tiles)]
        for r in range(local)
    ]
    limits = [
        [
            jnp.where(t < count_ref[r], kpt_ref[jnp.clip(cov_ref[r, t], 0, kpt_ref.shape[0] - 1)], 0)
            for t in range(tiles)
        ]
        for r in range(local)
    ]
    biases = [
        [jnp.where(lanes < limits[r][t], 0.0, DEAD) for t in range(tiles)] for r in range(local)
    ]

    for r in range(local):
        keys = jnp.concatenate([near_k[near_ids[r][t]] for t in range(tiles)], axis=0)
        values = jnp.concatenate([near_v[near_ids[r][t]] for t in range(tiles)], axis=0)
        q = query[r]
        bias = jnp.concatenate(biases[r], axis=1)
        spans = [jnp.where(hit, q, jnp.zeros_like(q)) for hit in heads]
        stacked = lax.dot_general(
            jnp.concatenate(spans, axis=0),
            keys,
            (((1,), (1,)), ((), ())),
            preferred_element_type=jnp.float32,
        )
        message = jnp.zeros((block, width), jnp.float32)
        for head in range(HEADS):
            logits = stacked[head * block : (head + 1) * block] + bias
            weights = jnp.exp(logits - jnp.max(logits, axis=1, keepdims=True))
            inverse = 1.0 / jnp.sum(weights, axis=1, keepdims=True)
            out = jnp.dot(
                weights.astype(jnp.bfloat16), values, preferred_element_type=jnp.float32
            )
            message = jnp.where(heads[head], out * inverse, message)
        hidden = jnp.maximum(
            merged[r]
            + jnp.dot(
                message.astype(jnp.bfloat16),
                wm_ref[pl.ds(width, width), :],
                preferred_element_type=jnp.float32,
            ),
            0.0,
        ).astype(jnp.bfloat16)
        refined = desc_ref[r].astype(jnp.float32) + jnp.dot(
            hidden, wo_ref[...], preferred_element_type=jnp.float32
        )
        near_ref[group + blk * local + r] = refined.astype(jnp.bfloat16)

    own_slot = slot(near_ref, 1, blk)
    send_own(own_slot, near_ref, ref_ssem, ref_rsem)
    drain(desc_in, near_desc, desc_ssem, desc_rsem)
    for section in (0, 2):
        relay(near_ref, ref_ssem, ref_rsem, section)
    for section in (1, 0, 2):
        wait_relayed(near_ref, ref_ssem, ref_rsem, section)

    dust = dust_ref[0]
    row_live = [rows_at < own_kpt[r] for r in range(local)]
    for r in range(local):
        mine = near_ref[group + blk * local + r] * jnp.asarray(
            1.0 / math.sqrt(width), jnp.bfloat16
        )
        row_bias = jnp.where(row_live[r], 0.0, DEAD)
        for t in range(tiles):
            out = lax.dot_general(
                mine,
                near_ref[near_ids[r][t]],
                (((1,), (1,)), ((), ())),
                preferred_element_type=jnp.float32,
            )
            scores[r, t] = out + (row_bias + biases[r][t])

    slots = lax.broadcasted_iota(jnp.int32, (group, 1), 0)
    pots = [jnp.zeros((group, block), jnp.float32)] * 3

    def mass_copy(sweep, shift, member):
        first, count = max(0, shift), 3 - abs(shift)
        return pltpu.make_async_remote_copy(
            src_ref=acc.at[sweep, pl.ds(first, count)],
            dst_ref=mass_in.at[sweep, 2 - shift, blk, pl.ds(first, count)],
            send_sem=mass_ssem.at[sweep, shift + 2, member],
            recv_sem=mass_rsem.at[sweep, 2 - shift, blk],
            device_id=(img + shift, member),
            device_id_type=MESH,
        )

    def mass_arrival(sweep, source, member):
        first, count = max(0, -source), 3 - abs(source)
        here = mass_in.at[sweep, source + 2, member, pl.ds(first, count)]
        return pltpu.make_async_remote_copy(
            src_ref=here,
            dst_ref=here,
            send_sem=mass_ssem.at[sweep, source + 2, member],
            recv_sem=mass_rsem.at[sweep, source + 2, member],
            device_id=(img, others[0]),
            device_id_type=MESH,
        )

    def each_partner(body):
        for shift in (-1, 1, -2, 2, 0):
            def run(shift=shift):
                for member in others if shift == 0 else range(blk_count):
                    body(shift, member)
            guarded(shift, run)

    def base_copy(r, t):
        return pltpu.make_async_copy(scores.at[r, t], base_out.at[r, t], base_sem.at[r, t])

    row_pots = [None] * local
    for sweep in range(ITERS):
        spread = [jnp.zeros((group, block), jnp.float32)] * 3
        for r in range(local):
            def shifted(t):
                if sweep == 0:
                    return scores[r, t]
                return scores[r, t] + pot[pl.ds(near_ids[r][t], 1), :]
            top = shifted(0)
            for t in range(1, tiles):
                top = jnp.maximum(top, shifted(t))
            top = jnp.maximum(jnp.max(top, axis=1, keepdims=True), dust)
            terms = [jnp.exp(shifted(t) - top) for t in range(tiles)]
            total = functools.reduce(jnp.add, terms)
            total = jnp.sum(total, axis=1, keepdims=True) + jnp.exp(dust - top)
            row_pots[r] = -(top + jnp.log(total))
            inverse = 1.0 / total
            for t in range(tiles):
                mass = jnp.sum(terms[t] * inverse, axis=0, keepdims=True)
                for section in range(3):
                    hit = slots == near_ids[r][t] - section * group
                    spread[section] = spread[section] + jnp.where(hit, mass, 0.0)
        for section in range(3):
            acc[sweep, section] = spread[section]
        each_partner(lambda shift, member: mass_copy(sweep, shift, member).start())
        if sweep == 0:
            drain(own_slot, near_ref, ref_ssem, ref_rsem)
        if sweep == ITERS - 1:
            for r in range(local):
                row = jnp.broadcast_to(row_pots[r], (block, block))
                row = jnp.sum(jnp.where(rows_at == lanes, row, 0.0), axis=0, keepdims=True)
                tail_ref[pl.ds(local * tiles + r, 1), :] = jnp.where(lanes < own_kpt[r], dust + row, 0.0)
                for t in range(tiles):
                    scores[r, t] = scores[r, t] + row_pots[r]
                    base_copy(r, t).start()
        sums = list(spread)
        each_partner(lambda source, member: mass_arrival(sweep, source, member).wait_recv())
        for source in range(-2, 3):
            for member in others if source == 0 else range(blk_count):
                for section in range(3):
                    if 0 <= section - source <= 2:
                        sums[section] = sums[section] + mass_in[
                            sweep, source + 2, member, section - source
                        ]
        for section in range(3):
            pots[section] = pots[section] - jnp.log(
                sums[section] + jnp.exp(dust + pots[section])
            )
            pot[pl.ds(section * group, group), :] = pots[section]

    for r in range(local):
        for t in range(tiles):
            tail_ref[pl.ds(r * tiles + t, 1), :] = pot[pl.ds(near_ids[r][t], 1), :]
        mine = pot[pl.ds(group + blk * local + r, 1), :]
        tail_ref[pl.ds(local * (tiles + 1) + r, 1), :] = jnp.where(lanes < own_kpt[r], dust + mine, 0.0)
    for sweep in range(ITERS):
        each_partner(lambda shift, member: mass_copy(sweep, shift, member).wait_send())
    for r in range(local):
        for t in range(tiles):
            base_copy(r, t).wait()


def finish(
    base_in, tail_in, plan_out, row_out, col_out, tail_ref, taken, made, in_sem, out_sem, end_sem
):
    local, tiles = base_in.shape[:2]
    places = [(r, t) for r in range(local) for t in range(tiles)]

    def fetch(r, t):
        return pltpu.make_async_copy(base_in.at[r, t], taken.at[r, t], in_sem.at[r, t])

    def put(r, t):
        return pltpu.make_async_copy(made.at[r, t], plan_out.at[r, t], out_sem.at[r, t])

    head = pltpu.make_async_copy(tail_in, tail_ref, end_sem.at[0])
    head.start()
    for place in places:
        fetch(*place).start()
    head.wait()
    ends = [
        pltpu.make_async_copy(
            tail_ref.at[pl.ds(local * (tiles + step), local)], target, end_sem.at[1 + step]
        )
        for step, target in enumerate((row_out, col_out))
    ]
    for end in ends:
        end.start()
    for r, t in places:
        fetch(r, t).wait()
        base = taken[r, t]
        out = base + tail_ref[pl.ds(r * tiles + t, 1), :]
        made[r, t] = jnp.where(base > 0.1 * DEAD, out, 0.0)
        put(r, t).start()
    for place in places:
        put(*place).wait()
    for end in ends:
        end.wait()


def on_device(
    img_count,
    blk_count,
    descriptors,
    covisible,
    tile_counts,
    keypoints,
    query_weight,
    key_weight,
    value_weight,
    merge_weight,
    output_weight,
    dustbin,
):
    local, block, width = descriptors.shape
    tiles = covisible.shape[1]
    group = local * blk_count
    near = 3 * group
    vmem = pl.BlockSpec(memory_space=pltpu.VMEM)
    hbm = pl.BlockSpec(memory_space=pltpu.HBM)
    dma = pltpu.SemaphoreType.DMA
    half = jnp.bfloat16
    full = jnp.float32
    base, tail = pl.pallas_call(
        functools.partial(kernel, img_count, blk_count),
        out_shape=(
            jax.ShapeDtypeStruct((local, tiles, block, block), full),
            jax.ShapeDtypeStruct((local * (tiles + 2), block), full),
        ),
        in_specs=[hbm] * 10,
        out_specs=(hbm, vmem),
        scratch_shapes=[
            pltpu.VMEM(descriptors.shape, half),
            pltpu.SMEM(covisible.shape, jnp.int32),
            pltpu.SMEM(tile_counts.shape, jnp.int32),
            pltpu.SMEM(keypoints.shape, jnp.int32),
            pltpu.VMEM(query_weight.shape, half),
            pltpu.VMEM(key_weight.shape, half),
            pltpu.VMEM(value_weight.shape, half),
            pltpu.VMEM(merge_weight.shape, half),
            pltpu.VMEM(output_weight.shape, half),
            pltpu.SMEM(dustbin.shape, full),
            dma((10,)),
            dma((descriptors.shape[0], tiles)),
            pltpu.VMEM((near, block, width), half),
            pltpu.VMEM((near, block, width), half),
            pltpu.VMEM((near, block, width), half),
            pltpu.VMEM((near, block, width), half),
            pltpu.VMEM((local, block, width), half),
            pltpu.VMEM((local, block, merge_weight.shape[1]), full),
            pltpu.VMEM((local, tiles, block, block), full),
            pltpu.VMEM((ITERS, 3, group, block), full),
            pltpu.VMEM((ITERS, 5, blk_count, 3, group, block), full),
            pltpu.VMEM((near, block), full),
            dma((3, blk_count)),
            dma((3, blk_count)),
            dma((3, blk_count)),
            dma((3, blk_count)),
            dma((ITERS, 5, blk_count)),
            dma((ITERS, 5, blk_count)),
        ],
        compiler_params=pltpu.CompilerParams(
            collective_id=0, has_side_effects=True
        ),
    )(
        descriptors,
        covisible,
        tile_counts,
        keypoints,
        query_weight,
        key_weight,
        value_weight,
        merge_weight,
        output_weight,
        dustbin,
    )
    return pl.pallas_call(
        finish,
        out_shape=(
            jax.ShapeDtypeStruct(base.shape, full),
            jax.ShapeDtypeStruct((local, block), full),
            jax.ShapeDtypeStruct((local, block), full),
        ),
        in_specs=[hbm, hbm],
        out_specs=(hbm, hbm, hbm),
        scratch_shapes=[
            pltpu.VMEM(tail.shape, full),
            pltpu.VMEM(base.shape, full),
            pltpu.VMEM(base.shape, full),
            dma((local, tiles)),
            dma((local, tiles)),
            dma((3,)),
        ],
    )(base, tail)


def solution(mesh):
    in_specs = (
        P(("img", "blk"), None, None),
        P(("img", "blk"), None),
        P(("img", "blk")),
        P(),
        P(),
        P(),
        P(),
        P(),
        P(),
        P(),
    )
    out_specs = (
        P(("img", "blk"), None, None, None),
        P(("img", "blk"), None),
        P(("img", "blk"), None),
    )
    return jax.shard_map(
        functools.partial(on_device, mesh.shape["img"], mesh.shape["blk"]),
        mesh=mesh,
        in_specs=in_specs,
        out_specs=out_specs,
        check_vma=False,
    )
```

profile of v0, /device:TPU:0, one launch (start us, length us, event | category | flops | bytes accessed | tf_op | source)
XLA Modules:
  0.0 39.5 jit_solution(8582232265168315056)
XLA Ops:
  1.3 36.1 %shard_map.121 = (f32[2,6,128,128]{3,2,1,0:T(8,128)}, f32[16,128]{1,0:T(8,128)}) custom-call(bf16[2,128,256]{2,1,0:T(8,128)(2,1)} %desc_in.1, s32[2,6]{1,0:T(2,128)} %cov_in.1, s32[2]{0:T(128)} %count_in.1, s32[64]{0:T(128)} %kpt_in.1, bf16[256,256]{1,0:T(8,128)(2,1)} %wq_in.1, bf16[256,256]{1,0:T(8,128)(2,1)} %wk_in.1, bf16[256,256]{1,0:T(8,128)(2,1)} %wv_in.1, ...), custom_call_target="tpu_custom_call" | custom-call | tf_op jit(solution)/shard_map/pallas_call | solution.py:452
  37.4 2.1 %shard_map.122 = (f32[2,6,128,128]{3,2,1,0:T(8,128)}, f32[2,128]{1,0:T(2,128)}, f32[2,128]{1,0:T(2,128)}) custom-call(f32[2,6,128,128]{3,2,1,0:T(8,128)} %get-tuple-element.5.base_in, f32[16,128]{1,0:T(8,128)} %get-tuple-element.6.tail_in), custom_call_target="tpu_custom_call" | custom-call | tf_op jit(solution)/shard_map/pallas_call | solution.py:505
where the time goes:
time: 39.7 us; the launch traced here: 39.5 us
  Pallas kernels  38.3 us (96%)
  between operations  1.29 us (3%)
    pallas_call x1, Pallas kernels, on_device(): pl.pallas_call(functools.partial(kernel, img_count, blk_count), out_shape...  36.1 us
    pallas_call x1, Pallas kernels, on_device(): pl.pallas_call(finish, out_shape=(jax.ShapeDtypeStruct(base.shape, full),...  2.12 us

commit v1 on v0

--- a/solution.py
+++ b/solution.py
@@ -12,6 +12,7 @@
 ITERS = 3
 DEAD = -1e30
 MESH = pl.DeviceIdType.MESH
+VMEM_BYTES = 32 * 1024 * 1024
 
 
 def kernel(
@@ -27,7 +28,7 @@
     wm_in,
     wo_in,
     dust_in,
-    base_out,
+    scores,
     tail_ref,
     desc_ref,
     cov_ref,
@@ -40,14 +41,12 @@
     wo_ref,
     dust_ref,
     load_sem,
-    base_sem,
     near_desc,
     near_ref,
     near_k,
     near_v,
     query,
     merged,
-    scores,
     acc,
     mass_in,
     pot,
@@ -323,9 +322,6 @@
                 for member in others if shift == 0 else range(blk_count):
                     body(shift, member)
             guarded(shift, run)
-
-    def base_copy(r, t):
-        return pltpu.make_async_copy(scores.at[r, t], base_out.at[r, t], base_sem.at[r, t])
 
     row_pots = [None] * local
     for sweep in range(ITERS):
@@ -361,7 +357,6 @@
                 tail_ref[pl.ds(local * tiles + r, 1), :] = jnp.where(lanes < own_kpt[r], dust + row, 0.0)
                 for t in range(tiles):
                     scores[r, t] = scores[r, t] + row_pots[r]
-                    base_copy(r, t).start()
         sums = list(spread)
         each_partner(lambda source, member: mass_arrival(sweep, source, member).wait_recv())
         for source in range(-2, 3):
@@ -384,39 +379,25 @@
         tail_ref[pl.ds(local * (tiles + 1) + r, 1), :] = jnp.where(lanes < own_kpt[r], dust + mine, 0.0)
     for sweep in range(ITERS):
         each_partner(lambda shift, member: mass_copy(sweep, shift, member).wait_send())
-    for r in range(local):
-        for t in range(tiles):
-            base_copy(r, t).wait()
-
-
-def finish(
-    base_in, tail_in, plan_out, row_out, col_out, tail_ref, taken, made, in_sem, out_sem, end_sem
-):
-    local, tiles = base_in.shape[:2]
+
+
+def finish(base_ref, tail_ref, plan_out, row_out, col_out, made, out_sem, end_sem):
+    local, tiles = base_ref.shape[:2]
     places = [(r, t) for r in range(local) for t in range(tiles)]
-
-    def fetch(r, t):
-        return pltpu.make_async_copy(base_in.at[r, t], taken.at[r, t], in_sem.at[r, t])
 
     def put(r, t):
         return pltpu.make_async_copy(made.at[r, t], plan_out.at[r, t], out_sem.at[r, t])
 
-    head = pltpu.make_async_copy(tail_in, tail_ref, end_sem.at[0])
-    head.start()
-    for place in places:
-        fetch(*place).start()
-    head.wait()
     ends = [
         pltpu.make_async_copy(
-            tail_ref.at[pl.ds(local * (tiles + step), local)], target, end_sem.at[1 + step]
+            tail_ref.at[pl.ds(local * (tiles + step), local)], target, end_sem.at[step]
         )
         for step, target in enumerate((row_out, col_out))
     ]
     for end in ends:
         end.start()
     for r, t in places:
-        fetch(r, t).wait()
-        base = taken[r, t]
+        base = base_ref[r, t]
         out = base + tail_ref[pl.ds(r * tiles + t, 1), :]
         made[r, t] = jnp.where(base > 0.1 * DEAD, out, 0.0)
         put(r, t).start()
@@ -452,11 +433,11 @@
     base, tail = pl.pallas_call(
         functools.partial(kernel, img_count, blk_count),
         out_shape=(
-            jax.ShapeDtypeStruct((local, tiles, block, block), full),
-            jax.ShapeDtypeStruct((local * (tiles + 2), block), full),
+            pltpu.VMEM((local, tiles, block, block), full),
+            pltpu.VMEM((local * (tiles + 2), block), full),
         ),
         in_specs=[hbm] * 10,
-        out_specs=(hbm, vmem),
+        out_specs=(vmem, vmem),
         scratch_shapes=[
             pltpu.VMEM(descriptors.shape, half),
             pltpu.SMEM(covisible.shape, jnp.int32),
@@ -469,14 +450,12 @@
             pltpu.VMEM(output_weight.shape, half),
             pltpu.SMEM(dustbin.shape, full),
             dma((10,)),
-            dma((descriptors.shape[0], tiles)),
             pltpu.VMEM((near, block, width), half),
             pltpu.VMEM((near, block, width), half),
             pltpu.VMEM((near, block, width), half),
             pltpu.VMEM((near, block, width), half),
             pltpu.VMEM((local, block, width), half),
             pltpu.VMEM((local, block, merge_weight.shape[1]), full),
-            pltpu.VMEM((local, tiles, block, block), full),
             pltpu.VMEM((ITERS, 3, group, block), full),
             pltpu.VMEM((ITERS, 5, blk_count, 3, group, block), full),
             pltpu.VMEM((near, block), full),
@@ -488,18 +467,23 @@
             dma((ITERS, 5, blk_count)),
         ],
         compiler_params=pltpu.CompilerParams(
-            collective_id=0, has_side_effects=True
+            collective_id=0, has_side_effects=True, vmem_limit_bytes=VMEM_BYTES
         ),
     )(
-        descriptors,
-        covisible,
-        tile_counts,
-        keypoints,
-        query_weight,
-        key_weight,
-        value_weight,
-        merge_weight,
-        output_weight,
+        *(
+            pltpu.with_memory_space_constraint(x, pltpu.HBM)
+            for x in (
+                descriptors,
+                covisible,
+                tile_counts,
+                keypoints,
+                query_weight,
+                key_weight,
+                value_weight,
+                merge_weight,
+                output_weight,
+            )
+        ),
         dustbin,
     )
     return pl.pallas_call(
@@ -509,17 +493,15 @@
             jax.ShapeDtypeStruct((local, block), full),
             jax.ShapeDtypeStruct((local, block), full),
         ),
-        in_specs=[hbm, hbm],
+        in_specs=[vmem, vmem],
         out_specs=(hbm, hbm, hbm),
         scratch_shapes=[
-            pltpu.VMEM(tail.shape, full),
-            pltpu.VMEM(base.shape, full),
             pltpu.VMEM(base.shape, full),
             dma((local, tiles)),
-            dma((local, tiles)),
-            dma((3,)),
+            dma((2,)),
         ],
-    )(base, tail)
+        compiler_params=pltpu.CompilerParams(vmem_limit_bytes=VMEM_BYTES),
+    )(*(pltpu.with_memory_space_constraint(x, pltpu.VMEM) for x in (base, tail)))
 
 
 def solution(mesh):

time: 39.7 us -> 37.9 us (0.955)
  Pallas kernels: 38.3 us -> 36.4 us
    pallas_call x1, Pallas kernels: 2.12 us -> 1.01 us  [on_device(): pl.pallas_call(finish, out_shape=(jax.ShapeDtypeStruct(base.shape, full),...]
    pallas_call x1, Pallas kernels: 36.1 us -> 35.4 us  [on_device(): pl.pallas_call(functools.partial(kernel, img_count, blk_count), out_shape...]
where the time goes in v1:
time: 37.9 us; the launch traced here: 37.7 us
  Pallas kernels  36.4 us (96%)
  between operations  1.29 us (3%)
    pallas_call x1, Pallas kernels, on_device(): pl.pallas_call(functools.partial(kernel, img_count, blk_count), out_shape...  35.4 us
    pallas_call x1, Pallas kernels, on_device(): pl.pallas_call(finish, out_shape=(jax.ShapeDtypeStruct(base.shape, full),...  1.01 us

profile of v1, /device:TPU:0, one launch (start us, length us, event | category | flops | bytes accessed | tf_op | source)
XLA Modules:
  0.0 37.7 jit_solution(13491686685360284102)
XLA Ops:
  1.3 35.4 %shard_map.121 = (f32[2,6,128,128]{3,2,1,0:T(8,128)S(1)}, f32[16,128]{1,0:T(8,128)S(1)}) custom-call(bf16[2,128,256]{2,1,0:T(8,128)(2,1)} %desc_in.1, s32[2,6]{1,0:T(2,128)} %cov_in.1, s32[2]{0:T(128)} %count_in.1, s32[64]{0:T(128)} %kpt_in.1, bf16[256,256]{1,0:T(8,128)(2,1)} %wq_in.1, bf16[256,256]{1,0:T(8,128)(2,1)} %wk_in.1, bf16[256,256]{1,0:T(8,128)(2,1)} %wv_in.1, ...), custom_call_target="tpu_custom_call" | custom-call | tf_op jit(solution)/shard_map/pallas_call | solution.py:433
  36.7 1.0 %shard_map.122 = (f32[2,6,128,128]{3,2,1,0:T(8,128)}, f32[2,128]{1,0:T(2,128)}, f32[2,128]{1,0:T(2,128)}) custom-call(f32[2,6,128,128]{3,2,1,0:T(8,128)S(1)} %get-tuple-element.5.base_ref, f32[16,128]{1,0:T(8,128)S(1)} %get-tuple-element.6.tail_ref), custom_call_target="tpu_custom_call" | custom-call | tf_op jit(solution)/shard_map/pallas_call | solution.py:489

commit v2 on v1

v2 whole, which is shorter than its diff:
```python
import functools
import math

import jax
import jax.numpy as jnp
from jax import lax
from jax.experimental import pallas as pl
from jax.experimental.pallas import tpu as pltpu
from jax.sharding import PartitionSpec as P

HEADS = 4
ITERS = 3
DEAD = -1e30
MESH = pl.DeviceIdType.MESH
VMEM_BYTES = 48 * 1024 * 1024


def kernel(
    img_count,
    blk_count,
    desc_in,
    cov_in,
    count_in,
    kpt_in,
    wq_in,
    wk_in,
    wv_in,
    wm_in,
    wo_in,
    dust_in,
    scores,
    tail_ref,
    desc_ref,
    cov_ref,
    count_ref,
    kpt_ref,
    dust_ref,
    weights_ref,
    load_sem,
    near_desc,
    near_ref,
    value_turned,
    spans,
    merged,
    slot_limit,
    top_ref,
    sum_ref,
    mix_ref,
    logit_ref,
    dots,
    acc,
    mass_in,
    pot,
    send_sem,
    pair_sem,
    direct_sem,
    passed_sem,
    mass_ssem,
    mass_rsem,
):
    local, block, width = desc_ref.shape
    tiles = cov_ref.shape[1]
    group = local * blk_count
    head_dim = width // HEADS
    deep = wm_in.shape[1]
    img = lax.axis_index("img")
    blk = lax.axis_index("blk")
    others = [lax.rem(blk + step, blk_count) for step in range(1, blk_count)]
    first_block = (img - 1) * group
    far = 2 * lax.rem(img, 2) - 1
    near = -far

    def exists(shift):
        if isinstance(shift, int):
            return img + shift < img_count if shift > 0 else img + shift >= 0
        return jnp.logical_and(img + shift >= 0, img + shift < img_count)

    has_far, has_near = exists(far), exists(near)

    sizes = (width, width, width, deep)
    starts = [sum(sizes[:place]) for place in range(len(sizes) + 1)]
    weight_rows = [(wq_in, 0), (wk_in, 0), (wv_in, 0), (wo_in, 0)]
    weight_rows += [(wm_in, column) for column in range(0, deep, width)]
    loads = []
    start = 0
    for source, column in weight_rows:
        count = source.shape[0]
        loads.append(
            pltpu.make_async_copy(
                source.at[:, pl.ds(column, width)],
                weights_ref.at[pl.ds(start, count)],
                load_sem.at[0],
            )
        )
        start += count
    weight_load = pltpu.make_async_copy(weights_ref, weights_ref, load_sem.at[0])
    small_loads = [
        pltpu.make_async_copy(source, target, load_sem.at[1 + place])
        for place, (source, target) in enumerate(
            (
                (desc_in, desc_ref),
                (cov_in, cov_ref),
                (count_in, count_ref),
                (kpt_in, kpt_ref),
                (dust_in, dust_ref),
            )
        )
    ]

    def weight(place):
        return weights_ref[pl.ds(starts[place], sizes[place]), :]

    def merge_part(step, column):
        first = starts[4] + column * 2 * width + step * width
        return weights_ref[pl.ds(first, width), :]

    barrier = pltpu.get_barrier_semaphore()

    def greet(shift, member):
        pl.semaphore_signal(
            barrier, inc=1, device_id=(img + shift, member), device_id_type=MESH
        )

    for shift in (far, near):
        pl.when(exists(shift))(lambda shift=shift: greet(shift, blk))
    for member in others:
        greet(0, member)

    for load in small_loads + loads:
        load.start()

    def slot_of(section, member, place):
        return (section * blk_count + member) * local + place

    def push(phase, source, slot, rsem, device):
        room = (near_desc, near_ref)[phase]
        pltpu.make_async_remote_copy(
            src_ref=source,
            dst_ref=room.at[slot],
            send_sem=send_sem.at[phase],
            recv_sem=rsem,
            device_id=device,
            device_id_type=MESH,
        ).start()

    def received(phase, rsem, first, count):
        room = (near_desc, near_ref)[phase]
        here = room.at[pl.ds(first, count)]
        pltpu.make_async_remote_copy(
            src_ref=here,
            dst_ref=here,
            send_sem=send_sem.at[phase],
            recv_sem=rsem,
            device_id=(img, others[0]),
            device_id_type=MESH,
        ).wait_recv()

    sides = ((has_far, far), (has_near, near))

    def send_own(phase, source):
        for place in range(local):
            for member in others:
                push(
                    phase,
                    source(place),
                    slot_of(1, blk, place),
                    pair_sem.at[phase],
                    (img, member),
                )
        for order, (there, shift) in enumerate(sides):
            @pl.when(there)
            def _(order=order, shift=shift):
                for place in range(local):
                    push(
                        phase,
                        source(place),
                        slot_of(1 - shift, blk, place),
                        direct_sem.at[phase, order, place],
                        (img + shift, blk),
                    )

    def collect(phase, use):
        room = (near_desc, near_ref)[phase]
        count = len(others)

        def relay(order, place):
            slot = slot_of(1 + sides[order][1], blk, place)
            received(phase, direct_sem.at[phase, order, place], slot, 1)
            for member in others:
                push(
                    phase, room.at[slot], slot, passed_sem.at[phase, order, place], (img, member)
                )

        def piece(order, place):
            section = 1 + sides[order][1]
            first = slot_of(section, others[0], place) if count == 1 else 0
            received(phase, passed_sem.at[phase, order, place], first, count)
            use([slot_of(section, member, place) for member in range(blk_count)])

        first = slot_of(1, others[0], 0) if count == 1 else 0
        received(phase, pair_sem.at[phase], first, count * local)
        use([slot_of(1, member, place) for member in others for place in range(local)])

        @pl.when(has_far)
        def _():
            for place in range(local):
                relay(0, place)
            for place in range(local - 1):
                piece(0, place)

        @pl.when(has_near)
        def _():
            for place in range(local - 1):
                relay(1, place)

        @pl.when(has_far)
        def _():
            piece(0, local - 1)

        @pl.when(has_near)
        def _():
            relay(1, local - 1)
            for place in range(local):
                piece(1, place)

    def drain(phase):
        for with_far in (False, True):
            for with_near in (False, True):
                count = local * len(others)
                count += (with_far + with_near) * local * (1 + len(others))

                @pl.when(jnp.logical_and(has_far == with_far, has_near == with_near))
                def _(count=count):
                    here = near_ref.at[pl.ds(0, count)]
                    pltpu.make_async_remote_copy(
                        src_ref=here,
                        dst_ref=here,
                        send_sem=send_sem.at[phase],
                        recv_sem=send_sem.at[phase],
                        device_id=(img, others[0]),
                        device_id_type=MESH,
                    ).wait_send()

    def mass_at(source, member):
        count = 3 - abs(source)
        base = {0: 0, -1: 3, 1: 5, -2: 7, 2: 8}[source] * blk_count
        return base + member * count, count

    for source in range(-2, 3):
        if source != 0:
            @pl.when(jnp.logical_not(exists(source)))
            def _(source=source):
                first = mass_at(source, 0)[0]
                count = mass_at(source, blk_count)[0] - first
                for sweep in range(ITERS):
                    mass_in[sweep, pl.ds(first, count)] = jnp.zeros(
                        (count, group, block), jnp.float32
                    )
    for source in (-1, 1):
        @pl.when(jnp.logical_not(exists(source)))
        def _(source=source):
            for r in range(local):
                for spot in range(group):
                    dots[r, (1 + source) * group + spot] = jnp.zeros((block, block), jnp.float32)

    pl.semaphore_wait(
        barrier, len(others) + has_far.astype(jnp.int32) + has_near.astype(jnp.int32)
    )
    send_own(0, lambda place: desc_in.at[place])
    for load in small_loads:
        load.wait()
    weight_load.wait()

    lanes = lax.broadcasted_iota(jnp.int32, (1, block), 1)
    rows_at = lax.broadcasted_iota(jnp.int32, (block, 1), 0)
    head_of = lax.broadcasted_iota(jnp.int32, (1, width), 1) // head_dim
    own_kpt = [kpt_ref[(img * blk_count + blk) * local + r] for r in range(local)]
    near_ids = [
        [jnp.clip(cov_ref[r, t] - first_block, 0, 3 * group - 1) for t in range(tiles)]
        for r in range(local)
    ]
    limits = [
        [
            jnp.where(t < count_ref[r], kpt_ref[jnp.clip(cov_ref[r, t], 0, kpt_ref.shape[0] - 1)], 0)
            for t in range(tiles)
        ]
        for r in range(local)
    ]
    biases = [
        [jnp.where(lanes < limits[r][t], 0.0, DEAD) for t in range(tiles)] for r in range(local)
    ]
    for r in range(local):
        for spot in range(3 * group):
            limit = 0
            for t in range(tiles):
                limit = jnp.where(near_ids[r][t] == spot, limits[r][t], limit)
            slot_limit[r, spot] = limit

    own = desc_ref[...].reshape(local * block, width)
    query = jnp.dot(own, weight(0), preferred_element_type=jnp.float32).astype(jnp.bfloat16)
    for r in range(local):
        q = query[r * block : (r + 1) * block]
        turned = lax.dot_general(
            jnp.concatenate(
                [jnp.where(head_of == head, q, jnp.zeros_like(q)) for head in range(HEADS)], axis=0
            ),
            weight(1),
            (((1,), (1,)), ((), ())),
            preferred_element_type=jnp.float32,
        )
        spans[r] = (turned * (math.log2(math.e) / math.sqrt(head_dim))).astype(jnp.bfloat16)
    value_turned[...] = weight(2).T
    columns = deep // width
    for column in range(columns):
        merged[:, pl.ds(column * width, width)] = jnp.dot(
            own, merge_part(0, column), preferred_element_type=jnp.float32
        )
    places_at = lax.broadcasted_iota(jnp.int32, (block, block), 0)
    step_heads = 2 if HEADS % 2 == 0 else 1

    def attend(rows, spots, first=False):
        values = lax.dot_general(
            value_turned[...], rows, (((1,), (1,)), ((), ())), preferred_element_type=jnp.float32
        ).astype(jnp.bfloat16)
        lives = [[places_at < slot_limit[r, spot] for spot in spots] for r in range(local)]
        chains = [(r, base) for r in range(local) for base in range(0, HEADS, step_heads)]

        def compare(chain):
            r, base = chain
            logits = lax.dot_general(
                rows,
                spans[r, pl.ds(base * block, step_heads * block)],
                (((1,), (1,)), ((), ())),
                preferred_element_type=jnp.float32,
            )
            tops = []
            for head in range(step_heads):
                top = None
                for place, alive in enumerate(lives[r]):
                    where_to = (pl.ds(place * block, block), pl.ds(head * block, block))
                    part = jnp.where(
                        alive,
                        logits[
                            place * block : (place + 1) * block,
                            head * block : (head + 1) * block,
                        ],
                        DEAD,
                    )
                    logit_ref[r, base // step_heads, where_to[0], where_to[1]] = part
                    top = part if top is None else jnp.maximum(top, part)
                tops.append(jnp.max(top, axis=0, keepdims=True))
            return tops

        def soften(chain, logits):
            r, base = chain
            weights = []
            scales = []
            for head in range(step_heads):
                where_to = pl.ds(base + head, 1)
                parts = [
                    logit_ref[
                        r,
                        base // step_heads,
                        pl.ds(place * block, block),
                        pl.ds(head * block, block),
                    ]
                    for place in range(len(spots))
                ]
                top = logits[head]
                if not first:
                    old = top_ref[r, where_to, :]
                    top = jnp.maximum(top, old)
                    scales.append(jnp.exp2(old - top))
                parts = [jnp.exp2(part - top) for part in parts]
                total = jnp.sum(functools.reduce(jnp.add, parts), axis=0, keepdims=True)
                if not first:
                    total = total + sum_ref[r, where_to, :] * scales[head]
                top_ref[r, where_to, :] = top
                sum_ref[r, where_to, :] = total
                weights.append(
                    jnp.concatenate([part.astype(jnp.bfloat16) for part in parts], axis=0)
                )
            return jnp.concatenate(weights, axis=1), scales

        def blend(chain, weights, scales):
            r, base = chain
            out = jnp.dot(
                values[base * head_dim : (base + step_heads) * head_dim],
                weights,
                preferred_element_type=jnp.float32,
            )
            for head in range(step_heads):
                where_to = pl.ds((base + head) * head_dim, head_dim)
                mix = out[
                    head * head_dim : (head + 1) * head_dim, head * block : (head + 1) * block
                ]
                if not first:
                    mix = mix + mix_ref[r, where_to, :] * scales[head]
                mix_ref[r, where_to, :] = mix

        compared = [compare(chain) for chain in chains]
        softened = [soften(chain, logits) for chain, logits in zip(chains, compared)]
        for chain, soft in zip(chains, softened):
            blend(chain, *soft)

    def attend_near(spots):
        attend(jnp.concatenate([near_desc[spot] for spot in spots], axis=0), spots)

    attend(own, [slot_of(1, blk, place) for place in range(local)], first=True)
    collect(0, attend_near)

    message = jnp.concatenate(
        [
            jnp.concatenate(
                [
                    mix_ref[r, pl.ds(head * head_dim, head_dim), :]
                    * (1.0 / sum_ref[r, pl.ds(head, 1), :])
                    for head in range(HEADS)
                ],
                axis=0,
            )
            for r in range(local)
        ],
        axis=1,
    ).astype(jnp.bfloat16)
    refined = desc_ref[...].reshape(local * block, width).astype(jnp.float32)
    for column in range(columns):
        hidden = jnp.maximum(
            merged[:, pl.ds(column * width, width)]
            + lax.dot_general(
                message,
                merge_part(1, column),
                (((0,), (0,)), ((), ())),
                preferred_element_type=jnp.float32,
            ),
            0.0,
        ).astype(jnp.bfloat16)
        refined = refined + jnp.dot(
            hidden,
            weights_ref[pl.ds(starts[3] + column * width, width), :],
            preferred_element_type=jnp.float32,
        )
    refined = refined.astype(jnp.bfloat16)
    near_ref[pl.ds(slot_of(1, blk, 0), local)] = refined.reshape(local, block, width)
    send_own(1, lambda place: near_ref.at[slot_of(1, blk, place)])

    mine = refined * jnp.asarray(1.0 / math.sqrt(width), jnp.bfloat16)

    def multiply(spots):
        theirs = jnp.concatenate([near_ref[spot] for spot in spots], axis=0)
        out = lax.dot_general(
            mine, theirs, (((1,), (1,)), ((), ())), preferred_element_type=jnp.float32
        )
        for r in range(local):
            for place, spot in enumerate(spots):
                dots[r, spot] = out[
                    r * block : (r + 1) * block, place * block : (place + 1) * block
                ]

    multiply([slot_of(1, blk, place) for place in range(local)])
    collect(1, multiply)

    dust = dust_ref[0]
    row_live = [rows_at < own_kpt[r] for r in range(local)]
    row_bias = [jnp.where(row_live[r], 0.0, DEAD) for r in range(local)]

    slots = lax.broadcasted_iota(jnp.int32, (group, 1), 0)
    pots = [jnp.zeros((group, block), jnp.float32)] * 3

    def mass_start(sweep, shift, member):
        first, count = mass_at(-shift, blk)
        pltpu.make_async_remote_copy(
            src_ref=acc.at[sweep, pl.ds(max(0, shift), count)],
            dst_ref=mass_in.at[sweep, pl.ds(first, count)],
            send_sem=mass_ssem.at[sweep],
            recv_sem=mass_rsem.at[sweep],
            device_id=(img + shift, member),
            device_id_type=MESH,
        ).start()

    def mass_wait(sweep, wait):
        for below in range(3):
            for above in range(3):
                count = 3 * len(others)
                for reach in (below, above):
                    count += sum((3 - step) * blk_count for step in range(1, reach + 1))

                @pl.when(
                    jnp.logical_and(
                        jnp.minimum(img, 2) == below,
                        jnp.minimum(img_count - 1 - img, 2) == above,
                    )
                )
                def _(count=count):
                    here = mass_in.at[sweep, pl.ds(0, count)]
                    wait(
                        pltpu.make_async_remote_copy(
                            src_ref=here,
                            dst_ref=here,
                            send_sem=mass_ssem.at[sweep],
                            recv_sem=mass_rsem.at[sweep],
                            device_id=(img, others[0]),
                            device_id_type=MESH,
                        )
                    )

    def each_partner(body):
        for shift in (-1, 1, -2, 2):
            def run(shift=shift):
                for member in range(blk_count):
                    body(shift, member)
            pl.when(exists(shift))(run)
        for member in others:
            body(0, member)

    row_pots = [None] * local
    for sweep in range(ITERS):
        spread = [jnp.zeros((group, block), jnp.float32)] * 3
        for r in range(local):
            if sweep == 0:
                for t in range(tiles):
                    scores[r, t] = dots[r, near_ids[r][t]] + (row_bias[r] + biases[r][t])

            def shifted(t):
                if sweep == 0:
                    return scores[r, t]
                return scores[r, t] + pot[pl.ds(near_ids[r][t], 1), :]
            top = shifted(0)
            for t in range(1, tiles):
                top = jnp.maximum(top, shifted(t))
            top = jnp.maximum(jnp.max(top, axis=1, keepdims=True), dust)
            terms = [jnp.exp(shifted(t) - top) for t in range(tiles)]
            total = functools.reduce(jnp.add, terms)
            total = jnp.sum(total, axis=1, keepdims=True) + jnp.exp(dust - top)
            row_pots[r] = -(top + jnp.log(total))
            inverse = 1.0 / total
            for t in range(tiles):
                mass = jnp.sum(terms[t] * inverse, axis=0, keepdims=True)
                for section in range(3):
                    hit = slots == near_ids[r][t] - section * group
                    spread[section] = spread[section] + jnp.where(hit, mass, 0.0)
        for section in range(3):
            acc[sweep, section] = spread[section]
        each_partner(lambda shift, member: mass_start(sweep, shift, member))
        if sweep == 0:
            drain(0)
            drain(1)
        if sweep == ITERS - 1:
            for r in range(local):
                row = jnp.broadcast_to(row_pots[r], (block, block))
                row = jnp.sum(jnp.where(rows_at == lanes, row, 0.0), axis=0, keepdims=True)
                tail_ref[pl.ds(local * tiles + r, 1), :] = jnp.where(lanes < own_kpt[r], dust + row, 0.0)
                for t in range(tiles):
                    scores[r, t] = scores[r, t] + row_pots[r]
        sums = list(spread)
        mass_wait(sweep, lambda copy: copy.wait_recv())
        for source in range(-2, 3):
            for member in others if source == 0 else range(blk_count):
                for section in range(max(0, source), 3 + min(0, source)):
                    first, _ = mass_at(source, member)
                    sums[section] = sums[section] + mass_in[
                        sweep, first + section - max(0, source)
                    ]
        for section in range(3):
            pots[section] = pots[section] - jnp.log(
                sums[section] + jnp.exp(dust + pots[section])
            )
            pot[pl.ds(section * group, group), :] = pots[section]

    for r in range(local):
        for t in range(tiles):
            tail_ref[pl.ds(r * tiles + t, 1), :] = pot[pl.ds(near_ids[r][t], 1), :]
        mine = pot[pl.ds(group + blk * local + r, 1), :]
        tail_ref[pl.ds(local * (tiles + 1) + r, 1), :] = jnp.where(lanes < own_kpt[r], dust + mine, 0.0)
    for sweep in range(ITERS):
        mass_wait(sweep, lambda copy: copy.wait_send())


def finish(base_ref, tail_ref, plan_out, row_out, col_out, made, out_sem, end_sem):
    local, tiles = base_ref.shape[:2]
    places = [(r, t) for r in range(local) for t in range(tiles)]

    def put(r, t):
        return pltpu.make_async_copy(made.at[r, t], plan_out.at[r, t], out_sem)

    ends = [
        pltpu.make_async_copy(
            tail_ref.at[pl.ds(local * (tiles + step), local)], target, end_sem.at[step]
        )
        for step, target in enumerate((row_out, col_out))
    ]
    for end in ends:
        end.start()
    for r, t in places:
        base = base_ref[r, t]
        out = base + tail_ref[pl.ds(r * tiles + t, 1), :]
        made[r, t] = jnp.where(base > 0.1 * DEAD, out, 0.0)
        put(r, t).start()
    for end in ends:
        end.wait()
    pltpu.make_async_copy(made, plan_out, out_sem).wait()


def on_device(
    img_count,
    blk_count,
    descriptors,
    covisible,
    tile_counts,
    keypoints,
    query_weight,
    key_weight,
    value_weight,
    merge_weight,
    output_weight,
    dustbin,
):
    local, block, width = descriptors.shape
    tiles = covisible.shape[1]
    group = local * blk_count
    near = 3 * group
    most = max(local * (blk_count - 1), blk_count, local)
    pace = 2 if HEADS % 2 == 0 else 1
    weight_rows = (
        3 * width
        + output_weight.shape[0]
        + merge_weight.shape[0] * (merge_weight.shape[1] // width)
    )
    vmem = pl.BlockSpec(memory_space=pltpu.VMEM)
    hbm = pl.BlockSpec(memory_space=pltpu.HBM)
    dma = pltpu.SemaphoreType.DMA
    half = jnp.bfloat16
    full = jnp.float32
    base, tail = pl.pallas_call(
        functools.partial(kernel, img_count, blk_count),
        out_shape=(
            pltpu.VMEM((local, tiles, block, block), full),
            pltpu.VMEM((local * (tiles + 2), block), full),
        ),
        in_specs=[hbm] * 10,
        out_specs=(vmem, vmem),
        scratch_shapes=[
            pltpu.VMEM(descriptors.shape, half),
            pltpu.SMEM(covisible.shape, jnp.int32),
            pltpu.SMEM(tile_counts.shape, jnp.int32),
            pltpu.SMEM(keypoints.shape, jnp.int32),
            pltpu.SMEM(dustbin.shape, full),
            pltpu.VMEM((weight_rows, width), half),
            dma((6,)),
            pltpu.VMEM((near, block, width), half),
            pltpu.VMEM((near, block, width), half),
            pltpu.VMEM(value_weight.shape, half),
            pltpu.VMEM((local, HEADS * block, width), half),
            pltpu.VMEM((local * block, merge_weight.shape[1]), full),
            pltpu.SMEM((local, near), jnp.int32),
            pltpu.VMEM((local, HEADS, block), full),
            pltpu.VMEM((local, HEADS, block), full),
            pltpu.VMEM((local, width, block), full),
            pltpu.VMEM((local, HEADS // pace, most * block, pace * block), full),
            pltpu.VMEM((local, near, block, block), full),
            pltpu.VMEM((ITERS, 3, group, block), full),
            pltpu.VMEM((ITERS, 9 * blk_count, group, block), full),
            pltpu.VMEM((near, block), full),
            dma((2,)),
            dma((2,)),
            dma((2, 2, local)),
            dma((2, 2, local)),
            dma((ITERS,)),
            dma((ITERS,)),
        ],
        compiler_params=pltpu.CompilerParams(
            collective_id=0, has_side_effects=True, vmem_limit_bytes=VMEM_BYTES
        ),
    )(
        *(
            pltpu.with_memory_space_constraint(x, pltpu.HBM)
            for x in (
                descriptors,
                covisible,
                tile_counts,
                keypoints,
                query_weight,
                key_weight,
                value_weight,
                merge_weight,
                output_weight,
            )
        ),
        dustbin,
    )
    return pl.pallas_call(
        finish,
        out_shape=(
            jax.ShapeDtypeStruct(base.shape, full),
            jax.ShapeDtypeStruct((local, block), full),
            jax.ShapeDtypeStruct((local, block), full),
        ),
        in_specs=[vmem, vmem],
        out_specs=(hbm, hbm, hbm),
        scratch_shapes=[
            pltpu.VMEM(base.shape, full),
            dma,
            dma((2,)),
        ],
        compiler_params=pltpu.CompilerParams(vmem_limit_bytes=VMEM_BYTES),
    )(*(pltpu.with_memory_space_constraint(x, pltpu.VMEM) for x in (base, tail)))


def solution(mesh):
    in_specs = (
        P(("img", "blk"), None, None),
        P(("img", "blk"), None),
        P(("img", "blk")),
        P(),
        P(),
        P(),
        P(),
        P(),
        P(),
        P(),
    )
    out_specs = (
        P(("img", "blk"), None, None, None),
        P(("img", "blk"), None),
        P(("img", "blk"), None),
    )
    return jax.shard_map(
        functools.partial(on_device, mesh.shape["img"], mesh.shape["blk"]),
        mesh=mesh,
        in_specs=in_specs,
        out_specs=out_specs,
        check_vma=False,
    )
```

time: 37.9 us -> 34.7 us (0.916)
  Pallas kernels: 36.4 us -> 33.3 us
    pallas_call x1, Pallas kernels: 35.4 us -> 32.4 us  [on_device(): pl.pallas_call(functools.partial(kernel, img_count, blk_count), out_shape...]
where the time goes in v2:
time: 34.7 us; the launch traced here: 34.6 us
  Pallas kernels  33.3 us (96%)
  between operations  1.29 us (4%)
    pallas_call x1, Pallas kernels, on_device(): pl.pallas_call(functools.partial(kernel, img_count, blk_count), out_shape...  32.4 us
    pallas_call x1, Pallas kernels, on_device(): pl.pallas_call(finish, out_shape=(jax.ShapeDtypeStruct(base.shape, full),...  0.91 us

profile of v2, /device:TPU:0, one launch (start us, length us, event | category | flops | bytes accessed | tf_op | source)
XLA Modules:
  0.0 34.6 jit_solution(5465399963742119531)
XLA Ops:
  1.3 32.4 %shard_map.121 = (f32[2,6,128,128]{3,2,1,0:T(8,128)S(1)}, f32[16,128]{1,0:T(8,128)S(1)}) custom-call(bf16[2,128,256]{2,1,0:T(8,128)(2,1)} %desc_in.1, s32[2,6]{1,0:T(2,128)} %cov_in.1, s32[2]{0:T(128)} %count_in.1, s32[64]{0:T(128)} %kpt_in.1, bf16[256,256]{1,0:T(8,128)(2,1)} %wq_in.1, bf16[256,256]{1,0:T(8,128)(2,1)} %wk_in.1, bf16[256,256]{1,0:T(8,128)(2,1)} %wv_in.1, ...), custom_call_target="tpu_custom_call" | custom-call | tf_op jit(solution)/shard_map/pallas_call | solution.py:634
  33.7 0.9 %shard_map.122 = (f32[2,6,128,128]{3,2,1,0:T(8,128)}, f32[2,128]{1,0:T(2,128)}, f32[2,128]{1,0:T(2,128)}) custom-call(f32[2,6,128,128]{3,2,1,0:T(8,128)S(1)} %get-tuple-element.5.base_ref, f32[16,128]{1,0:T(8,128)S(1)} %get-tuple-element.6.tail_ref), custom_call_target="tpu_custom_call" | custom-call | tf_op jit(solution)/shard_map/pallas_call | solution.py:691

commit v3 on v2

--- a/solution.py
+++ b/solution.py
@@ -11,6 +11,8 @@
 HEADS = 4
 ITERS = 3
 DEAD = -1e30
+LOG2E = math.log2(math.e)
+LN2 = math.log(2.0)
 MESH = pl.DeviceIdType.MESH
 VMEM_BYTES = 48 * 1024 * 1024
 
@@ -48,6 +50,7 @@
     mix_ref,
     logit_ref,
     dots,
+    shifted,
     acc,
     mass_in,
     pot,
@@ -75,7 +78,12 @@
             return img + shift < img_count if shift > 0 else img + shift >= 0
         return jnp.logical_and(img + shift >= 0, img + shift < img_count)
 
-    has_far, has_near = exists(far), exists(near)
+    has_far = exists(far)
+    has_near = True if img_count % 2 == 0 else exists(near)
+
+    def when(condition):
+        return (lambda body: body()) if condition is True else pl.when(condition)
+
 
     sizes = (width, width, width, deep)
     starts = [sum(sizes[:place]) for place in range(len(sizes) + 1)]
@@ -121,8 +129,8 @@
             barrier, inc=1, device_id=(img + shift, member), device_id_type=MESH
         )
 
-    for shift in (far, near):
-        pl.when(exists(shift))(lambda shift=shift: greet(shift, blk))
+    when(has_far)(lambda: greet(far, blk))
+    when(has_near)(lambda: greet(near, blk))
     for member in others:
         greet(0, member)
 
@@ -168,7 +176,7 @@
                     (img, member),
                 )
         for order, (there, shift) in enumerate(sides):
-            @pl.when(there)
+            @when(there)
             def _(order=order, shift=shift):
                 for place in range(local):
                     push(
@@ -191,11 +199,14 @@
                     phase, room.at[slot], slot, passed_sem.at[phase, order, place], (img, member)
                 )
 
-        def piece(order, place):
+        def passed(order, place):
             section = 1 + sides[order][1]
             first = slot_of(section, others[0], place) if count == 1 else 0
             received(phase, passed_sem.at[phase, order, place], first, count)
-            use([slot_of(section, member, place) for member in range(blk_count)])
+            return [slot_of(section, member, place) for member in range(blk_count)]
+
+        def piece(order, place):
+            use(passed(order, place))
 
         first = slot_of(1, others[0], 0) if count == 1 else 0
         received(phase, pair_sem.at[phase], first, count * local)
@@ -208,7 +219,7 @@
             for place in range(local - 1):
                 piece(0, place)
 
-        @pl.when(has_near)
+        @when(has_near)
         def _():
             for place in range(local - 1):
                 relay(1, place)
@@ -217,15 +228,20 @@
         def _():
             piece(0, local - 1)
 
-        @pl.when(has_near)
+        @when(has_near)
         def _():
-            relay(1, local - 1)
-            for place in range(local):
-                piece(1, place)
+            last = local - 1
+            relay(1, last)
+            spots = [slot_of(1 + near, blk, last)]
+            for place in range(last):
+                spots += passed(1, place)
+            use(spots)
+            passed(1, last)
+            use([slot_of(1 + near, member, last) for member in others])
 
     def drain(phase):
         for with_far in (False, True):
-            for with_near in (False, True):
+            for with_near in (True,) if has_near is True else (False, True):
                 count = local * len(others)
                 count += (with_far + with_near) * local * (1 + len(others))
 
@@ -263,11 +279,12 @@
                 for spot in range(group):
                     dots[r, (1 + source) * group + spot] = jnp.zeros((block, block), jnp.float32)
 
+    small_loads[0].wait()
     pl.semaphore_wait(
-        barrier, len(others) + has_far.astype(jnp.int32) + has_near.astype(jnp.int32)
+        barrier, len(others) + jnp.int32(has_far) + jnp.int32(has_near)
     )
-    send_own(0, lambda place: desc_in.at[place])
-    for load in small_loads:
+    send_own(0, lambda place: desc_ref.at[place])
+    for load in small_loads[1:]:
         load.wait()
     weight_load.wait()
 
@@ -453,7 +470,7 @@
         )
         for r in range(local):
             for place, spot in enumerate(spots):
-                dots[r, spot] = out[
+                dots[r, spot] = LOG2E * out[
                     r * block : (r + 1) * block, place * block : (place + 1) * block
                 ]
 
@@ -461,6 +478,7 @@
     collect(1, multiply)
 
     dust = dust_ref[0]
+    dust2 = dust * LOG2E
     row_live = [rows_at < own_kpt[r] for r in range(local)]
     row_bias = [jnp.where(row_live[r], 0.0, DEAD) for r in range(local)]
 
@@ -517,22 +535,21 @@
     for sweep in range(ITERS):
         spread = [jnp.zeros((group, block), jnp.float32)] * 3
         for r in range(local):
-            if sweep == 0:
-                for t in range(tiles):
-                    scores[r, t] = dots[r, near_ids[r][t]] + (row_bias[r] + biases[r][t])
-
-            def shifted(t):
+            top = None
+            for t in range(tiles):
                 if sweep == 0:
-                    return scores[r, t]
-                return scores[r, t] + pot[pl.ds(near_ids[r][t], 1), :]
-            top = shifted(0)
-            for t in range(1, tiles):
-                top = jnp.maximum(top, shifted(t))
-            top = jnp.maximum(jnp.max(top, axis=1, keepdims=True), dust)
-            terms = [jnp.exp(shifted(t) - top) for t in range(tiles)]
+                    moved = dots[r, near_ids[r][t]] + (row_bias[r] + biases[r][t])
+                    scores[r, t] = moved
+                else:
+                    moved = scores[r, t] + pot[pl.ds(near_ids[r][t], 1), :]
+                    shifted[r, t] = moved
+                top = moved if t == 0 else jnp.maximum(top, moved)
+            held = scores if sweep == 0 else shifted
+            top = jnp.maximum(jnp.max(top, axis=1, keepdims=True), dust2)
+            terms = [jnp.exp2(held[r, t] - top) for t in range(tiles)]
             total = functools.reduce(jnp.add, terms)
-            total = jnp.sum(total, axis=1, keepdims=True) + jnp.exp(dust - top)
-            row_pots[r] = -(top + jnp.log(total))
+            total = jnp.sum(total, axis=1, keepdims=True) + jnp.exp2(dust2 - top)
+            row_pots[r] = -(top + jnp.log2(total))
             inverse = 1.0 / total
             for t in range(tiles):
                 mass = jnp.sum(terms[t] * inverse, axis=0, keepdims=True)
@@ -547,11 +564,11 @@
             drain(1)
         if sweep == ITERS - 1:
             for r in range(local):
-                row = jnp.broadcast_to(row_pots[r], (block, block))
+                row = jnp.broadcast_to(row_pots[r] * LN2, (block, block))
                 row = jnp.sum(jnp.where(rows_at == lanes, row, 0.0), axis=0, keepdims=True)
                 tail_ref[pl.ds(local * tiles + r, 1), :] = jnp.where(lanes < own_kpt[r], dust + row, 0.0)
                 for t in range(tiles):
-                    scores[r, t] = scores[r, t] + row_pots[r]
+                    scores[r, t] = (scores[r, t] + row_pots[r]) * LN2
         sums = list(spread)
         mass_wait(sweep, lambda copy: copy.wait_recv())
         for source in range(-2, 3):
@@ -562,10 +579,12 @@
                         sweep, first + section - max(0, source)
                     ]
         for section in range(3):
-            pots[section] = pots[section] - jnp.log(
-                sums[section] + jnp.exp(dust + pots[section])
+            pots[section] = pots[section] - jnp.log2(
+                sums[section] + jnp.exp2(dust2 + pots[section])
             )
-            pot[pl.ds(section * group, group), :] = pots[section]
+            pot[pl.ds(section * group, group), :] = (
+                pots[section] * LN2 if sweep == ITERS - 1 else pots[section]
+            )
 
     for r in range(local):
         for t in range(tiles):
@@ -619,7 +638,7 @@
     tiles = covisible.shape[1]
     group = local * blk_count
     near = 3 * group
-    most = max(local * (blk_count - 1), blk_count, local)
+    most = max(local * (blk_count - 1), (local - 1) * blk_count + 1, blk_count, local)
     pace = 2 if HEADS % 2 == 0 else 1
     weight_rows = (
         3 * width
@@ -658,6 +677,7 @@
             pltpu.VMEM((local, width, block), full),
             pltpu.VMEM((local, HEADS // pace, most * block, pace * block), full),
             pltpu.VMEM((local, near, block, block), full),
+            pltpu.VMEM((local, tiles, block, block), full),
             pltpu.VMEM((ITERS, 3, group, block), full),
             pltpu.VMEM((ITERS, 9 * blk_count, group, block), full),
             pltpu.VMEM((near, block), full),

time: 34.7 us -> 34.4 us (level)
  Pallas kernels: 33.3 us -> 32.9 us
    pallas_call x1, Pallas kernels: 32.4 us -> 32 us  [on_device(): pl.pallas_call(functools.partial(kernel, img_count, blk_count), out_shape...]
where the time goes in v3:
time: 34.4 us; the launch traced here: 34.2 us
  Pallas kernels  32.9 us (96%)
  between operations  1.29 us (4%)
    pallas_call x1, Pallas kernels, on_device(): pl.pallas_call(functools.partial(kernel, img_count, blk_count), out_shape...  32 us
    pallas_call x1, Pallas kernels, on_device(): pl.pallas_call(finish, out_shape=(jax.ShapeDtypeStruct(base.shape, full),...  0.91 us

profile of v3, /device:TPU:0, one launch (start us, length us, event | category | flops | bytes accessed | tf_op | source)
XLA Modules:
  0.0 34.2 jit_solution(7599816597806853401)
XLA Ops:
  1.3 32.0 %shard_map.121 = (f32[2,6,128,128]{3,2,1,0:T(8,128)S(1)}, f32[16,128]{1,0:T(8,128)S(1)}) custom-call(bf16[2,128,256]{2,1,0:T(8,128)(2,1)} %desc_in.1, s32[2,6]{1,0:T(2,128)} %cov_in.1, s32[2]{0:T(128)} %count_in.1, s32[64]{0:T(128)} %kpt_in.1, bf16[256,256]{1,0:T(8,128)(2,1)} %wq_in.1, bf16[256,256]{1,0:T(8,128)(2,1)} %wk_in.1, bf16[256,256]{1,0:T(8,128)(2,1)} %wv_in.1, ...), custom_call_target="tpu_custom_call" | custom-call | tf_op jit(solution)/shard_map/pallas_call | solution.py:653
  33.3 0.9 %shard_map.122 = (f32[2,6,128,128]{3,2,1,0:T(8,128)}, f32[2,128]{1,0:T(2,128)}, f32[2,128]{1,0:T(2,128)}) custom-call(f32[2,6,128,128]{3,2,1,0:T(8,128)S(1)} %get-tuple-element.5.base_ref, f32[16,128]{1,0:T(8,128)S(1)} %get-tuple-element.6.tail_ref), custom_call_target="tpu_custom_call" | custom-call | tf_op jit(solution)/shard_map/pallas_call | solution.py:711

commit v4 on v3

--- a/solution.py
+++ b/solution.py
@@ -110,7 +110,6 @@
                 (cov_in, cov_ref),
                 (count_in, count_ref),
                 (kpt_in, kpt_ref),
-                (dust_in, dust_ref),
             )
         )
     ]
@@ -477,7 +476,7 @@
     multiply([slot_of(1, blk, place) for place in range(local)])
     collect(1, multiply)
 
-    dust = dust_ref[0]
+    dust = dust_in[0]
     dust2 = dust * LOG2E
     row_live = [rows_at < own_kpt[r] for r in range(local)]
     row_bias = [jnp.where(row_live[r], 0.0, DEAD) for r in range(local)]
@@ -656,7 +655,7 @@
             pltpu.VMEM((local, tiles, block, block), full),
             pltpu.VMEM((local * (tiles + 2), block), full),
         ),
-        in_specs=[hbm] * 10,
+        in_specs=[hbm] * 9 + [pl.BlockSpec(memory_space=pltpu.SMEM)],
         out_specs=(vmem, vmem),
         scratch_shapes=[
             pltpu.VMEM(descriptors.shape, half),

time: 34.4 us -> 34.4 us (level)
  no operation moved by 1% of the time
where the time goes in v4:
time: 34.4 us; the launch traced here: 34.2 us
  Pallas kernels  32.9 us (96%)
  between operations  1.29 us (4%)
    pallas_call x1, Pallas kernels, on_device(): pl.pallas_call(functools.partial(kernel, img_count, blk_count), out_shape...  32 us
    pallas_call x1, Pallas kernels, on_device(): pl.pallas_call(finish, out_shape=(jax.ShapeDtypeStruct(base.shape, full),...  0.91 us

profile of v4, /device:TPU:0, one launch (start us, length us, event | category | flops | bytes accessed | tf_op | source)
XLA Modules:
  0.0 34.2 jit_solution(5327544731541279752)
XLA Ops:
  1.3 32.0 %shard_map.121 = (f32[2,6,128,128]{3,2,1,0:T(8,128)S(1)}, f32[16,128]{1,0:T(8,128)S(1)}) custom-call(bf16[2,128,256]{2,1,0:T(8,128)(2,1)} %desc_in.1, s32[2,6]{1,0:T(2,128)} %cov_in.1, s32[2]{0:T(128)} %count_in.1, s32[64]{0:T(128)} %kpt_in.1, bf16[256,256]{1,0:T(8,128)(2,1)} %wq_in.1, bf16[256,256]{1,0:T(8,128)(2,1)} %wk_in.1, bf16[256,256]{1,0:T(8,128)(2,1)} %wv_in.1, ...), custom_call_target="tpu_custom_call" | custom-call | tf_op jit(solution)/shard_map/pallas_call | solution.py:652
  33.3 0.9 %shard_map.122 = (f32[2,6,128,128]{3,2,1,0:T(8,128)}, f32[2,128]{1,0:T(2,128)}, f32[2,128]{1,0:T(2,128)}) custom-call(f32[2,6,128,128]{3,2,1,0:T(8,128)S(1)} %get-tuple-element.5.base_ref, f32[16,128]{1,0:T(8,128)S(1)} %get-tuple-element.6.tail_ref), custom_call_target="tpu_custom_call" | custom-call | tf_op jit(solution)/shard_map/pallas_call | solution.py:710

commit v5 on v4

--- a/solution.py
+++ b/solution.py
@@ -489,13 +489,13 @@
         pltpu.make_async_remote_copy(
             src_ref=acc.at[sweep, pl.ds(max(0, shift), count)],
             dst_ref=mass_in.at[sweep, pl.ds(first, count)],
-            send_sem=mass_ssem.at[sweep],
+            send_sem=mass_ssem.at[0],
             recv_sem=mass_rsem.at[sweep],
             device_id=(img + shift, member),
             device_id_type=MESH,
         ).start()
 
-    def mass_wait(sweep, wait):
+    def mass_wait(sweep):
         for below in range(3):
             for above in range(3):
                 count = 3 * len(others)
@@ -509,26 +509,40 @@
                     )
                 )
                 def _(count=count):
-                    here = mass_in.at[sweep, pl.ds(0, count)]
-                    wait(
-                        pltpu.make_async_remote_copy(
-                            src_ref=here,
-                            dst_ref=here,
-                            send_sem=mass_ssem.at[sweep],
-                            recv_sem=mass_rsem.at[sweep],
-                            device_id=(img, others[0]),
-                            device_id_type=MESH,
-                        )
+                    if sweep is None:
+                        here = mass_in.at[:, pl.ds(0, count)]
+                    else:
+                        here = mass_in.at[sweep, pl.ds(0, count)]
+                    copy = pltpu.make_async_remote_copy(
+                        src_ref=here,
+                        dst_ref=here,
+                        send_sem=mass_ssem.at[0],
+                        recv_sem=mass_rsem.at[0 if sweep is None else sweep],
+                        device_id=(img, others[0]),
+                        device_id_type=MESH,
                     )
+                    if sweep is None:
+                        copy.wait_send()
+                    else:
+                        copy.wait_recv()
+
+    inner = jnp.logical_and(exists(-2), exists(2))
 
     def each_partner(body):
-        for shift in (-1, 1, -2, 2):
-            def run(shift=shift):
-                for member in range(blk_count):
-                    body(shift, member)
-            pl.when(exists(shift))(run)
-        for member in others:
-            body(0, member)
+        def run(shift):
+            for member in others if shift == 0 else range(blk_count):
+                body(shift, member)
+
+        @pl.when(inner)
+        def _():
+            for shift in (-1, 1, -2, 2, 0):
+                run(shift)
+
+        @pl.when(jnp.logical_not(inner))
+        def _():
+            for shift in (-1, 1, -2, 2):
+                pl.when(exists(shift))(lambda shift=shift: run(shift))
+            run(0)
 
     row_pots = [None] * local
     for sweep in range(ITERS):
@@ -569,7 +583,7 @@
                 for t in range(tiles):
                     scores[r, t] = (scores[r, t] + row_pots[r]) * LN2
         sums = list(spread)
-        mass_wait(sweep, lambda copy: copy.wait_recv())
+        mass_wait(sweep)
         for source in range(-2, 3):
             for member in others if source == 0 else range(blk_count):
                 for section in range(max(0, source), 3 + min(0, source)):
@@ -590,8 +604,7 @@
             tail_ref[pl.ds(r * tiles + t, 1), :] = pot[pl.ds(near_ids[r][t], 1), :]
         mine = pot[pl.ds(group + blk * local + r, 1), :]
         tail_ref[pl.ds(local * (tiles + 1) + r, 1), :] = jnp.where(lanes < own_kpt[r], dust + mine, 0.0)
-    for sweep in range(ITERS):
-        mass_wait(sweep, lambda copy: copy.wait_send())
+    mass_wait(None)
 
 
 def finish(base_ref, tail_ref, plan_out, row_out, col_out, made, out_sem, end_sem):
@@ -684,7 +697,7 @@
             dma((2,)),
             dma((2, 2, local)),
             dma((2, 2, local)),
-            dma((ITERS,)),
+            dma((1,)),
             dma((ITERS,)),
         ],
         compiler_params=pltpu.CompilerParams(

time: 34.4 us -> 34.3 us (level)
  no operation moved by 1% of the time
where the time goes in v5:
time: 34.3 us; the launch traced here: 34.2 us
  Pallas kernels  32.9 us (96%)
  between operations  1.29 us (4%)
    pallas_call x1, Pallas kernels, on_device(): pl.pallas_call(functools.partial(kernel, img_count, blk_count), out_shape...  32 us
    pallas_call x1, Pallas kernels, on_device(): pl.pallas_call(finish, out_shape=(jax.ShapeDtypeStruct(base.shape, full),...  0.91 us

profile of v5, /device:TPU:0, one launch (start us, length us, event | category | flops | bytes accessed | tf_op | source)
XLA Modules:
  0.0 34.2 jit_solution(615508307641879441)
XLA Ops:
  1.3 32.0 %shard_map.121 = (f32[2,6,128,128]{3,2,1,0:T(8,128)S(1)}, f32[16,128]{1,0:T(8,128)S(1)}) custom-call(bf16[2,128,256]{2,1,0:T(8,128)(2,1)} %desc_in.1, s32[2,6]{1,0:T(2,128)} %cov_in.1, s32[2]{0:T(128)} %count_in.1, s32[64]{0:T(128)} %kpt_in.1, bf16[256,256]{1,0:T(8,128)(2,1)} %wq_in.1, bf16[256,256]{1,0:T(8,128)(2,1)} %wk_in.1, bf16[256,256]{1,0:T(8,128)(2,1)} %wv_in.1, ...), custom_call_target="tpu_custom_call" | custom-call | tf_op jit(solution)/shard_map/pallas_call | solution.py:665
  33.3 0.9 %shard_map.122 = (f32[2,6,128,128]{3,2,1,0:T(8,128)}, f32[2,128]{1,0:T(2,128)}, f32[2,128]{1,0:T(2,128)}) custom-call(f32[2,6,128,128]{3,2,1,0:T(8,128)S(1)} %get-tuple-element.5.base_ref, f32[16,128]{1,0:T(8,128)S(1)} %get-tuple-element.6.tail_ref), custom_call_target="tpu_custom_call" | custom-call | tf_op jit(solution)/shard_map/pallas_call | solution.py:723
